TPU v7x, 32 devices: a whole 2x2x4 slice. The times are simulated.
32 devices in a mesh: rows: 4 (over y, core), cols: 8 (over z, x).
Axes of the slice: x: 2, y: 2, z: 4, core: 2. Of those that a mesh axis runs over, the one named last changes fastest.
Arguments:
- object_field: float32 [2, 512, 1024], P(None, 'rows', 'cols'), may hold values from -6 to 6
- probe: float32 [2, 256, 256], replicated, may hold values from -6 to 6
- amplitudes: float32 [4, 8, 4, 256, 256], P('rows', 'cols'), may hold values from 0.5 to 4
- offsets: int32 [4, 8, 4, 2], P('rows', 'cols'), may hold values from 0 to 128
Outputs:
- updated: float32 [2, 512, 1024], P(None, 'rows', 'cols')
Inputs may be any that keep to these rules, and one draw needn't show every extreme that they name: `offsets`: every window lies inside its tile's extended region of 384 cells a side.
All inputs are finite; a program needn't handle non-finite values.
Results may differ from a plain program's by a relative error of at most 0.0001.
Values sent between devices are 32-bit elements; how exact they have to be, the bound alone decides.
No kernel may reach another device: no remote copies, remote signals or barrier semaphores. Data moves between devices by JAX's collectives and lax.ppermute only.
A program may use at most 64 MiB of HBM per device.

v0:
```python
import functools
import math

import jax
import jax.numpy as jnp
import numpy as np
from jax import lax
from jax.experimental import pallas as pl
from jax.experimental.pallas import tpu as pltpu
from jax.sharding import PartitionSpec as P

ITERS = 2
FLOOR = 0.5
f32 = jnp.float32
bf16 = jnp.bfloat16
VMEM = pl.BlockSpec(memory_space=pltpu.VMEM)
SMEM = pl.BlockSpec(memory_space=pltpu.SMEM)


def swap(value, axis, odd):
    n = lax.axis_size(axis)
    first = 1 if odd else 0
    pairs = []
    for i in range(first, n - 1, 2):
        pairs += [(i, i + 1), (i + 1, i)]
    return lax.ppermute(value, axis, pairs)


def dft_matrices(size):
    half = size // 2
    k = np.arange(half)[:, None]
    m = np.arange(half)[None, :]
    mats = []
    for odd in (0, 1):
        angle = 2.0 * np.pi / size * (((2 * k + odd) * m) % size)
        c = np.cos(angle) / math.sqrt(size)
        s = np.sin(angle) / math.sqrt(size)
        w = np.block([[c, s], [-s, c]])
        mats += [w, w.T]
    mats = np.stack(mats).astype(np.float32)
    hi = mats.astype(jnp.bfloat16)
    lo = (mats - hi.astype(np.float32)).astype(jnp.bfloat16)
    return np.stack([hi, lo])


def split(x):
    hi = x.astype(bf16)
    lo = (x - hi.astype(f32)).astype(bf16)
    return hi, lo


def times_right(x, mats, which):
    hi, lo = split(x)
    lhs = jnp.concatenate([hi, lo, hi], 1)
    rhs = jnp.concatenate([mats[0, which], mats[0, which], mats[1, which]], 0)
    return jnp.dot(lhs, rhs, preferred_element_type=f32)


def times_left(mats, which, x):
    hi, lo = split(x)
    lhs = jnp.concatenate([mats[0, which], mats[1, which], mats[0, which]], 1)
    rhs = jnp.concatenate([hi, hi, lo], 0)
    return jnp.dot(lhs, rhs, preferred_element_type=f32)


WE, WET, WO, WOT = 0, 1, 2, 3


def split_three(x):
    a = x.astype(bf16)
    rest = x - a.astype(f32)
    b = rest.astype(bf16)
    return [a, b, (rest - b.astype(f32)).astype(bf16)]


def amps_kernel(amps_ref, perm_ref, out_ref):
    perm = perm_ref[0]
    perm_t = perm_ref[1]
    for p in range(amps_ref.shape[0]):
        cols = jnp.dot(
            jnp.concatenate(split_three(amps_ref[p]), 1),
            jnp.concatenate([perm] * 3, 0),
            preferred_element_type=f32,
        )
        out_ref[p] = jnp.dot(
            jnp.concatenate([perm_t] * 3, 1),
            jnp.concatenate(split_three(cols), 0),
            preferred_element_type=f32,
        )


def place_at(x, shift, extent):
    rows = x.shape[0]
    wide = jnp.concatenate([x, jnp.zeros((rows, extent - x.shape[1]), f32)], 1)
    return pltpu.roll(wide, shift, 1)


def windows_kernel(
    with_light, flags_ref, offs_ref, strip_ref, even_ref, odd_ref, probe_ref, amps_ref,
    mats_ref, mid_ref, to_even_ref, to_odd_ref, ext, acc,
):
    own = strip_ref.shape[1]
    extent = 3 * own
    size = probe_ref.shape[1]
    half = size // 2
    positions = amps_ref.shape[0]
    parity = flags_ref[0]
    even_at = pl.multiple_of((1 - parity) * 2 * own, own)
    odd_at = pl.multiple_of(parity * 2 * own, own)
    for k in range(2):
        for j in range(3):
            lanes = slice(j * own, (j + 1) * own)
            ext[3 * k + j, own : 2 * own, :] = strip_ref[k, :, lanes]
            ext[3 * k + j, pl.ds(even_at, own), :] = even_ref[k, :, lanes]
            ext[3 * k + j, pl.ds(odd_at, own), :] = odd_ref[k, :, lanes]
    acc[...] = jnp.zeros_like(acc)
    mats = mats_ref

    def window_of(k, rows, back_by):
        wide = jnp.concatenate([ext[3 * k + j, rows, :] for j in range(3)], 1)
        return pltpu.roll(wide, back_by, 1)[:, :size]

    def add_at(k, rows, x, shift):
        wide = place_at(x, shift, extent)
        for j in range(3):
            acc[3 * k + j, rows, :] += wide[:, j * own : (j + 1) * own]

    def window(p):
        first = offs_ref[2 * p]
        second = offs_ref[2 * p + 1]
        back_by = jnp.where(second == 0, 0, extent - second)
        parts = []
        for h in (0, 1):
            rows = pl.ds(first + h * half, half)
            orr = window_of(0, rows, back_by)
            oi = window_of(1, rows, back_by)
            pr = probe_ref[0, h * half : (h + 1) * half, :]
            pi = probe_ref[1, h * half : (h + 1) * half, :]
            er = pr * orr - pi * oi
            ei = pr * oi + pi * orr
            s = jnp.concatenate([er[:, :half] + er[:, half:], ei[:, :half] + ei[:, half:]], 1)
            d = jnp.concatenate([er[:, :half] - er[:, half:], ei[:, :half] - ei[:, half:]], 1)
            parts.append((times_right(s, mats, WET), times_right(d, mats, WOT)))
        (te, to), (be, bo) = parts
        e_out = None
        outs = []
        for odd, (e, o) in enumerate(((te + be, to + bo), (te - be, to - bo))):
            x = jnp.concatenate(
                [
                    jnp.concatenate([e[:, :half], o[:, :half]], 1),
                    jnp.concatenate([e[:, half:], o[:, half:]], 1),
                ],
                0,
            )
            far = times_left(mats, WO if odd else WE, x)
            fr = far[:half]
            fi = far[half:]
            amp = amps_ref[p, odd * half : (odd + 1) * half, :]
            keep = 1.0 - amp * lax.rsqrt(jnp.maximum(fr * fr + fi * fi, FLOOR * FLOOR))
            y = jnp.concatenate([fr * keep, fi * keep], 0)
            outs.append(times_left(mats, WOT if odd else WET, y))
        e_out, o_out = outs
        for h in (0, 1):
            v = e_out + o_out if h == 0 else e_out - o_out
            le = jnp.concatenate([v[:half, :half], v[half:, :half]], 1)
            lo = jnp.concatenate([v[:half, half:], v[half:, half:]], 1)
            e = times_right(le, mats, WE)
            o = times_right(lo, mats, WO)
            u = e + o
            w = e - o
            br = jnp.concatenate([u[:, :half], w[:, :half]], 1)
            bi = jnp.concatenate([u[:, half:], w[:, half:]], 1)
            pr = probe_ref[0, h * half : (h + 1) * half, :]
            pi = probe_ref[1, h * half : (h + 1) * half, :]
            rows = pl.ds(first + h * half, half)
            add_at(0, rows, pr * br + pi * bi, second)
            add_at(1, rows, pr * bi - pi * br, second)
            if with_light:
                add_at(2, rows, pr * pr + pi * pi, second)

    for p in range(positions):
        window(p)
    for k in range(mid_ref.shape[0]):
        for j in range(3):
            lanes = slice(j * own, (j + 1) * own)
            mid_ref[k, :, lanes] = acc[3 * k + j, own : 2 * own, :]
            to_even_ref[k, :, lanes] = acc[3 * k + j, pl.ds(even_at, own), :]
            to_odd_ref[k, :, lanes] = acc[3 * k + j, pl.ds(odd_at, own), :]


def join_kernel(flags_ref, own_ref, even_ref, odd_ref, strip_ref):
    own = own_ref.shape[2]
    parity = flags_ref[1]
    strip_ref[:, :, own : 2 * own] = own_ref[...]

    @pl.when(parity == 0)
    def _():
        strip_ref[:, :, 2 * own :] = even_ref[...]
        strip_ref[:, :, :own] = odd_ref[...]

    @pl.when(parity == 1)
    def _():
        strip_ref[:, :, 2 * own :] = odd_ref[...]
        strip_ref[:, :, :own] = even_ref[...]


def rows_kernel(flags_ref, mid_ref, even_ref, odd_ref, keep_ref, to_even_ref, to_odd_ref):
    own = keep_ref.shape[2]
    parity = flags_ref[1]
    total = mid_ref[...] + even_ref[...] + odd_ref[...]
    keep_ref[...] = total[:, :, own : 2 * own]

    @pl.when(parity == 0)
    def _():
        to_even_ref[...] = total[:, :, 2 * own :]
        to_odd_ref[...] = total[:, :, :own]

    @pl.when(parity == 1)
    def _():
        to_even_ref[...] = total[:, :, :own]
        to_odd_ref[...] = total[:, :, 2 * own :]


def first_update_kernel(field_ref, keep_ref, even_ref, odd_ref, out_ref, light_ref):
    total = keep_ref[...] + even_ref[...] + odd_ref[...]
    light = total[2] + 1.0
    light_ref[...] = light
    out_ref[0] = field_ref[0] - total[0] / light
    out_ref[1] = field_ref[1] - total[1] / light


def update_kernel(field_ref, light_ref, keep_ref, even_ref, odd_ref, out_ref):
    total = keep_ref[...] + even_ref[...] + odd_ref[...]
    light = light_ref[...]
    out_ref[0] = field_ref[0] - total[0] / light
    out_ref[1] = field_ref[1] - total[1] / light


def call(kernel, shapes, specs, *args, scratch=(), flops=0):
    outs = [jax.ShapeDtypeStruct(s, f32) for s in shapes]
    moved = sum(a.size * a.dtype.itemsize for a in args)
    got = pl.pallas_call(
        kernel,
        out_shape=outs,
        in_specs=specs,
        out_specs=[VMEM] * len(outs),
        scratch_shapes=list(scratch),
        compiler_params=pltpu.CompilerParams(vmem_limit_bytes=40 * 2**20),
        cost_estimate=pl.CostEstimate(flops=flops, bytes_accessed=moved, transcendentals=0),
    )(*args)
    return got[0] if len(outs) == 1 else got


def local(object_field, probe, amplitudes, offsets):
    own = object_field.shape[1]
    size = probe.shape[1]
    positions = amplitudes.shape[2]
    extent = 3 * own
    amps = amplitudes.reshape(positions, size, size)
    offs = offsets.reshape(2 * positions)
    flags = jnp.stack([lax.axis_index("rows") % 2, lax.axis_index("cols") % 2]).astype(jnp.int32)
    mats = jnp.asarray(dft_matrices(size))
    order = np.concatenate([np.arange(0, size, 2), np.arange(1, size, 2)])
    perm = (np.arange(size)[:, None] == order[None, :]).astype(jnp.bfloat16)
    perm = jnp.asarray(np.stack([perm, perm.T]))
    amps = call(
        amps_kernel, [(positions, size, size)], [VMEM, VMEM], amps, perm,
        flops=6 * positions * size**3,
    )
    field = object_field
    light = None
    for step in range(ITERS):
        layers = 3 if step == 0 else 2
        strip = call(
            join_kernel, [(2, own, extent)], [SMEM] + [VMEM] * 3,
            flags, field, swap(field, "cols", False), swap(field, "cols", True),
        )
        mid, to_even, to_odd = call(
            functools.partial(windows_kernel, step == 0),
            [(layers, own, extent)] * 3,
            [SMEM, SMEM] + [VMEM] * 6,
            flags, offs, strip, swap(strip, "rows", False), swap(strip, "rows", True),
            probe, amps, mats,
            scratch=[pltpu.VMEM((3 * k, extent, own), f32) for k in (2, layers)],
            flops=48 * positions * size**3,
        )
        keep, to_even, to_odd = call(
            rows_kernel, [(layers, own, own)] * 3, [SMEM] + [VMEM] * 3,
            flags, mid, swap(to_even, "rows", False), swap(to_odd, "rows", True),
        )
        even, odd = swap(to_even, "cols", False), swap(to_odd, "cols", True)
        if step == 0:
            field, light = call(
                first_update_kernel, [(2, own, own), (own, own)], [VMEM] * 4,
                field, keep, even, odd,
            )
        else:
            field = call(
                update_kernel, [(2, own, own)], [VMEM] * 5, field, light, keep, even, odd
            )
    return field


def solution(mesh):
    placed = (
        P(None, "rows", "cols"),
        P(),
        P("rows", "cols", None, None, None),
        P("rows", "cols", None, None),
    )
    return jax.shard_map(
        local, mesh=mesh, in_specs=placed, out_specs=P(None, "rows", "cols"), check_vma=False
    )
```

profile of v0, /device:TPU:20, one launch (start us, length us, event | category | flops | bytes accessed | tf_op | source)
XLA Modules:
  0.0 99.0 jit_solution(1092547847849171919)
XLA Ops:
  0.0 3.3 %collective-permute-start.1 = (f32[2,128,128]{2,1,0:T(8,128)}, f32[2,128,128]{2,1,0:T(8,128)S(1)}, u32[]{:S(2)}, u32[]{:S(2)}) collective-permute-start(f32[2,128,128]{2,1,0:T(8,128)} %field_ref.1), channel_id=1, source_target_pairs={{1,2},{2,1},{3,4},{4,3},{5,6},{6,5},{9,10},{10,9},{11,12},{12,11},... | collective-permute-start | bytes 393224 | tf_op jit(solution)/shard_map/ppermute | solution.py:26
  3.3 1.7 %collective-permute-start = (f32[2,128,128]{2,1,0:T(8,128)}, f32[2,128,128]{2,1,0:T(8,128)S(1)}, u32[]{:S(2)}, u32[]{:S(2)}) collective-permute-start(f32[2,128,128]{2,1,0:T(8,128)} %field_ref.1), channel_id=1, source_target_pairs={{0,1},{1,0},{2,3},{3,2},{4,5},{5,4},{6,7},{7,6},{8,9},{9,8},{10,11... | collective-permute-start | bytes 393224 | tf_op jit(solution)/shard_map/ppermute | solution.py:26
  5.1 3.2 %collective-permute-done.1.odd_ref = f32[2,128,128]{2,1,0:T(8,128)S(1)} collective-permute-done((f32[2,128,128]{2,1,0:T(8,128)}, f32[2,128,128]{2,1,0:T(8,128)S(1)}, u32[]{:S(2)}, u32[]{:S(2)}) %collective-permute-start.1) | collective-permute-done | bytes 131104 | tf_op jit(solution)/shard_map/ppermute | solution.py:26
  8.3 2.7 %collective-permute-done.even_ref = f32[2,128,128]{2,1,0:T(8,128)S(1)} collective-permute-done((f32[2,128,128]{2,1,0:T(8,128)}, f32[2,128,128]{2,1,0:T(8,128)S(1)}, u32[]{:S(2)}, u32[]{:S(2)}) %collective-permute-start) | collective-permute-done | bytes 131104 | tf_op jit(solution)/shard_map/ppermute | solution.py:26
  12.5 2.0 %collective-permute-start.3 = (f32[2,128,384]{2,1,0:T(8,128)S(1)}, f32[2,128,384]{2,1,0:T(8,128)S(1)}, u32[]{:S(2)}, u32[]{:S(2)}) collective-permute-start(f32[2,128,384]{2,1,0:T(8,128)S(1)} %shard_map.64.strip_ref), channel_id=1, source_target_pairs={{8,16},{16,8},{9,17},{17,9},{10,18},{18,10},{11,19},{19,11},{12,20... | collective-permute-start | bytes 1179656 | tf_op jit(solution)/shard_map/ppermute | solution.py:26
  17.4 4.3 %collective-permute-done.3.odd_ref = f32[2,128,384]{2,1,0:T(8,128)S(1)} collective-permute-done((f32[2,128,384]{2,1,0:T(8,128)S(1)}, f32[2,128,384]{2,1,0:T(8,128)S(1)}, u32[]{:S(2)}, u32[]{:S(2)}) %collective-permute-start.3) | collective-permute-done | bytes 393248 | tf_op jit(solution)/shard_map/ppermute | solution.py:26
  21.6 8.1 %shard_map.66 = (f32[3,128,384]{2,1,0:T(8,128)S(1)}, f32[3,128,384]{2,1,0:T(8,128)S(1)}, f32[3,128,384]{2,1,0:T(8,128)S(1)}) custom-call(s32[2]{0:T(128)S(1)} %pad_add_fusion.flags_ref, s32[8]{0:T(128)S(1)} %reshape.6.offs_ref, f32[2,128,384]{2,1,0:T(8,128)S(1)} %shard_map.64.strip_ref, f32[2,128,384]{2,1,0:T(8,128)S(1)} %collective-permute-done.2.even_ref, ...), custom_call_target="tpu_custom_call" | custom-call | flops 3221225472 | bytes 3801128 | tf_op jit(solution)/shard_map/pallas_call | solution.py:242
  29.8 2.1 %collective-permute-start.5 = (f32[3,128,384]{2,1,0:T(8,128)S(1)}, f32[3,128,384]{2,1,0:T(8,128)S(1)}, u32[]{:S(2)}, u32[]{:S(2)}) collective-permute-start(f32[3,128,384]{2,1,0:T(8,128)S(1)} %get-tuple-element.21), channel_id=1, source_target_pairs={{8,16},{16,8},{9,17},{17,9},{10,18},{18,10},{11,19},{19,11},{12,20... | collective-permute-start | bytes 1769480 | tf_op jit(solution)/shard_map/ppermute | solution.py:26
  31.9 9.1 %collective-permute-done.5.odd_ref = f32[3,128,384]{2,1,0:T(8,128)S(1)} collective-permute-done((f32[3,128,384]{2,1,0:T(8,128)S(1)}, f32[3,128,384]{2,1,0:T(8,128)S(1)}, u32[]{:S(2)}, u32[]{:S(2)}) %collective-permute-start.5) | collective-permute-done | bytes 589856 | tf_op jit(solution)/shard_map/ppermute | solution.py:26
  41.7 1.6 %collective-permute-start.6 = (f32[3,128,128]{2,1,0:T(8,128)S(1)}, f32[3,128,128]{2,1,0:T(8,128)S(1)}, u32[]{:S(2)}, u32[]{:S(2)}) collective-permute-start(f32[3,128,128]{2,1,0:T(8,128)S(1)} %get-tuple-element.23), channel_id=1, source_target_pairs={{0,1},{1,0},{2,3},{3,2},{4,5},{5,4},{6,7},{7,6},{8,9},{9,8},{10,11... | collective-permute-start | bytes 589832 | tf_op jit(solution)/shard_map/ppermute | solution.py:26
  43.3 2.3 %collective-permute-start.7 = (f32[3,128,128]{2,1,0:T(8,128)S(1)}, f32[3,128,128]{2,1,0:T(8,128)S(1)}, u32[]{:S(2)}, u32[]{:S(2)}) collective-permute-start(f32[3,128,128]{2,1,0:T(8,128)S(1)} %get-tuple-element.24), channel_id=1, source_target_pairs={{1,2},{2,1},{3,4},{4,3},{5,6},{6,5},{9,10},{10,9},{11,12},{12,11},... | collective-permute-start | bytes 589832 | tf_op jit(solution)/shard_map/ppermute | solution.py:26
  45.6 6.7 %collective-permute-done.6.even_ref = f32[3,128,128]{2,1,0:T(8,128)S(1)} collective-permute-done((f32[3,128,128]{2,1,0:T(8,128)S(1)}, f32[3,128,128]{2,1,0:T(8,128)S(1)}, u32[]{:S(2)}, u32[]{:S(2)}) %collective-permute-start.6) | collective-permute-done | bytes 196640 | tf_op jit(solution)/shard_map/ppermute | solution.py:26
  52.4 3.3 %collective-permute-start.9 = (f32[2,128,128]{2,1,0:T(8,128)S(1)}, f32[2,128,128]{2,1,0:T(8,128)S(1)}, u32[]{:S(2)}, u32[]{:S(2)}) collective-permute-start(f32[2,128,128]{2,1,0:T(8,128)S(1)} %get-tuple-element.25.own_ref.field_ref), channel_id=1, source_target_pairs={{1,2},{2,1},{3,4},{4,3},{5,6},{6,5},{9,10},{10,9},{11,12},{12,11},... | collective-permute-start | bytes 393224 | tf_op jit(solution)/shard_map/ppermute | solution.py:26
  55.7 1.7 %collective-permute-start.8 = (f32[2,128,128]{2,1,0:T(8,128)S(1)}, f32[2,128,128]{2,1,0:T(8,128)S(1)}, u32[]{:S(2)}, u32[]{:S(2)}) collective-permute-start(f32[2,128,128]{2,1,0:T(8,128)S(1)} %get-tuple-element.25.own_ref.field_ref), channel_id=1, source_target_pairs={{0,1},{1,0},{2,3},{3,2},{4,5},{5,4},{6,7},{7,6},{8,9},{9,8},{10,11... | collective-permute-start | bytes 393224 | tf_op jit(solution)/shard_map/ppermute | solution.py:26
  57.5 2.8 %collective-permute-done.9.odd_ref = f32[2,128,128]{2,1,0:T(8,128)S(1)} collective-permute-done((f32[2,128,128]{2,1,0:T(8,128)S(1)}, f32[2,128,128]{2,1,0:T(8,128)S(1)}, u32[]{:S(2)}, u32[]{:S(2)}) %collective-permute-start.9) | collective-permute-done | bytes 131104 | tf_op jit(solution)/shard_map/ppermute | solution.py:26
  62.1 2.1 %collective-permute-start.11 = (f32[2,128,384]{2,1,0:T(8,128)S(1)}, f32[2,128,384]{2,1,0:T(8,128)S(1)}, u32[]{:S(2)}, u32[]{:S(2)}) collective-permute-start(f32[2,128,384]{2,1,0:T(8,128)S(1)} %shard_map.69.strip_ref), channel_id=1, source_target_pairs={{8,16},{16,8},{9,17},{17,9},{10,18},{18,10},{11,19},{19,11},{12,20... | collective-permute-start | bytes 1179656 | tf_op jit(solution)/shard_map/ppermute | solution.py:26
  64.3 6.9 %collective-permute-done.11.odd_ref = f32[2,128,384]{2,1,0:T(8,128)S(1)} collective-permute-done((f32[2,128,384]{2,1,0:T(8,128)S(1)}, f32[2,128,384]{2,1,0:T(8,128)S(1)}, u32[]{:S(2)}, u32[]{:S(2)}) %collective-permute-start.11) | collective-permute-done | bytes 393248 | tf_op jit(solution)/shard_map/ppermute | solution.py:26
  71.2 7.9 %shard_map.70 = (f32[2,128,384]{2,1,0:T(8,128)S(1)}, f32[2,128,384]{2,1,0:T(8,128)S(1)}, f32[2,128,384]{2,1,0:T(8,128)S(1)}) custom-call(s32[2]{0:T(128)S(1)} %pad_add_fusion.flags_ref, s32[8]{0:T(128)S(1)} %reshape.6.offs_ref, f32[2,128,384]{2,1,0:T(8,128)S(1)} %shard_map.69.strip_ref, f32[2,128,384]{2,1,0:T(8,128)S(1)} %collective-permute-done.10.even_ref, ...), custom_call_target="tpu_custom_call" | custom-call | flops 3221225472 | bytes 3801128 | tf_op jit(solution)/shard_map/pallas_call | solution.py:242
  79.2 1.9 %collective-permute-start.13 = (f32[2,128,384]{2,1,0:T(8,128)S(1)}, f32[2,128,384]{2,1,0:T(8,128)S(1)}, u32[]{:S(2)}, u32[]{:S(2)}) collective-permute-start(f32[2,128,384]{2,1,0:T(8,128)S(1)} %get-tuple-element.29), channel_id=1, source_target_pairs={{8,16},{16,8},{9,17},{17,9},{10,18},{18,10},{11,19},{19,11},{12,20... | collective-permute-start | bytes 1179656 | tf_op jit(solution)/shard_map/ppermute | solution.py:26
  81.1 7.1 %collective-permute-done.13.odd_ref = f32[2,128,384]{2,1,0:T(8,128)S(1)} collective-permute-done((f32[2,128,384]{2,1,0:T(8,128)S(1)}, f32[2,128,384]{2,1,0:T(8,128)S(1)}, u32[]{:S(2)}, u32[]{:S(2)}) %collective-permute-start.13) | collective-permute-done | bytes 393248 | tf_op jit(solution)/shard_map/ppermute | solution.py:26
  88.9 1.6 %collective-permute-start.14 = (f32[2,128,128]{2,1,0:T(8,128)S(1)}, f32[2,128,128]{2,1,0:T(8,128)S(1)}, u32[]{:S(2)}, u32[]{:S(2)}) collective-permute-start(f32[2,128,128]{2,1,0:T(8,128)S(1)} %get-tuple-element.31), channel_id=1, source_target_pairs={{0,1},{1,0},{2,3},{3,2},{4,5},{5,4},{6,7},{7,6},{8,9},{9,8},{10,11... | collective-permute-start | bytes 393224 | tf_op jit(solution)/shard_map/ppermute | solution.py:26
  90.5 1.9 %collective-permute-start.15 = (f32[2,128,128]{2,1,0:T(8,128)S(1)}, f32[2,128,128]{2,1,0:T(8,128)S(1)}, u32[]{:S(2)}, u32[]{:S(2)}) collective-permute-start(f32[2,128,128]{2,1,0:T(8,128)S(1)} %get-tuple-element.32), channel_id=1, source_target_pairs={{1,2},{2,1},{3,4},{4,3},{5,6},{6,5},{9,10},{10,9},{11,12},{12,11},... | collective-permute-start | bytes 393224 | tf_op jit(solution)/shard_map/ppermute | solution.py:26
  92.4 1.5 %collective-permute-done.14.even_ref = f32[2,128,128]{2,1,0:T(8,128)S(1)} collective-permute-done((f32[2,128,128]{2,1,0:T(8,128)S(1)}, f32[2,128,128]{2,1,0:T(8,128)S(1)}, u32[]{:S(2)}, u32[]{:S(2)}) %collective-permute-start.14) | collective-permute-done | bytes 131104 | tf_op jit(solution)/shard_map/ppermute | solution.py:26
  93.9 4.3 %collective-permute-done.15.odd_ref = f32[2,128,128]{2,1,0:T(8,128)S(1)} collective-permute-done((f32[2,128,128]{2,1,0:T(8,128)S(1)}, f32[2,128,128]{2,1,0:T(8,128)S(1)}, u32[]{:S(2)}, u32[]{:S(2)}) %collective-permute-start.15) | collective-permute-done | bytes 131104 | tf_op jit(solution)/shard_map/ppermute | solution.py:26
  (34 shorter events, 8.5 us)
Async XLA Ops:
  0.0 8.3 %collective-permute-start.1 = (f32[2,128,128]{2,1,0:T(8,128)}, f32[2,128,128]{2,1,0:T(8,128)S(1)}, u32[]{:S(2)}, u32[]{:S(2)}) collective-permute-start(f32[2,128,128]{2,1,0:T(8,128)} %field_ref.1), channel_id=1, source_target_pairs={{1,2},{2,1},{3,4},{4,3},{5,6},{6,5},{9,10},{10,9},{11,12},{12,11},... | collective-permute-start | bytes 393224 | tf_op jit(solution)/shard_map/ppermute | solution.py:26
  3.3 7.8 %collective-permute-start = (f32[2,128,128]{2,1,0:T(8,128)}, f32[2,128,128]{2,1,0:T(8,128)S(1)}, u32[]{:S(2)}, u32[]{:S(2)}) collective-permute-start(f32[2,128,128]{2,1,0:T(8,128)} %field_ref.1), channel_id=1, source_target_pairs={{0,1},{1,0},{2,3},{3,2},{4,5},{5,4},{6,7},{7,6},{8,9},{9,8},{10,11... | collective-permute-start | bytes 393224 | tf_op jit(solution)/shard_map/ppermute | solution.py:26
  5.0 9.6 %copy-start.6 = (s32[1,1,4,2]{2,3,1,0:T(2,128)S(1)}, s32[1,1,4,2]{2,3,1,0:T(2,128)}, u32[]{:S(2)}) copy-start(s32[1,1,4,2]{2,3,1,0:T(2,128)} %param.9) | copy-start | bytes 100
  11.0 0.9 copy-start.1
  11.9 2.9 %copy-start.3 = (bf16[2,256,256]{2,1,0:T(8,128)(2,1)S(1)}, bf16[2,256,256]{2,1,0:T(8,128)(2,1)}, u32[]{:S(2)}) copy-start(bf16[2,256,256]{2,1,0:T(8,128)(2,1)} %constant.30.clone.perm_ref) | copy-start | bytes 786436
  12.5 9.1 %collective-permute-start.3 = (f32[2,128,384]{2,1,0:T(8,128)S(1)}, f32[2,128,384]{2,1,0:T(8,128)S(1)}, u32[]{:S(2)}, u32[]{:S(2)}) collective-permute-start(f32[2,128,384]{2,1,0:T(8,128)S(1)} %shard_map.64.strip_ref), channel_id=1, source_target_pairs={{8,16},{16,8},{9,17},{17,9},{10,18},{18,10},{11,19},{19,11},{12,20... | collective-permute-start | bytes 1179656 | tf_op jit(solution)/shard_map/ppermute | solution.py:26
  14.6 7.1 %collective-permute-start.2 = (f32[2,128,384]{2,1,0:T(8,128)S(1)}, f32[2,128,384]{2,1,0:T(8,128)S(1)}, u32[]{:S(2)}, u32[]{:S(2)}) collective-permute-start(f32[2,128,384]{2,1,0:T(8,128)S(1)} %shard_map.64.strip_ref), channel_id=1, source_target_pairs={{0,8},{8,0},{16,24},{24,16},{1,9},{9,1},{17,25},{25,17},{2,10},{10... | collective-permute-start | bytes 1179656 | tf_op jit(solution)/shard_map/ppermute | solution.py:26
  14.8 1.2 %copy-start = (f32[1,1,4,256,256]{4,3,2,1,0:T(8,128)S(1)}, f32[1,1,4,256,256]{4,3,2,1,0:T(8,128)}, u32[]{:S(2)}) copy-start(f32[1,1,4,256,256]{4,3,2,1,0:T(8,128)} %param.8) | copy-start | bytes 3145732
  16.1 5.6 %copy-start.4 = (f32[2,256,256]{2,1,0:T(8,128)S(1)}, f32[2,256,256]{2,1,0:T(8,128)}, u32[]{:S(2)}) copy-start(f32[2,256,256]{2,1,0:T(8,128)} %probe_ref.3) | copy-start | bytes 1572868
  16.1 5.6 %copy-start.5 = (bf16[2,4,256,256]{3,2,1,0:T(8,128)(2,1)S(1)}, bf16[2,4,256,256]{3,2,1,0:T(8,128)(2,1)}, u32[]{:S(2)}) copy-start(bf16[2,4,256,256]{3,2,1,0:T(8,128)(2,1)} %constant.29.clone.mats_ref) | copy-start | bytes 3145732
  29.7 2.2 %collective-permute-start.4 = (f32[3,128,384]{2,1,0:T(8,128)S(1)}, f32[3,128,384]{2,1,0:T(8,128)S(1)}, u32[]{:S(2)}, u32[]{:S(2)}) collective-permute-start(f32[3,128,384]{2,1,0:T(8,128)S(1)} %get-tuple-element.20), channel_id=1, source_target_pairs={{0,8},{8,0},{16,24},{24,16},{1,9},{9,1},{17,25},{25,17},{2,10},{10... | collective-permute-start | bytes 1769480 | tf_op jit(solution)/shard_map/ppermute | solution.py:26
  29.8 11.2 %collective-permute-start.5 = (f32[3,128,384]{2,1,0:T(8,128)S(1)}, f32[3,128,384]{2,1,0:T(8,128)S(1)}, u32[]{:S(2)}, u32[]{:S(2)}) collective-permute-start(f32[3,128,384]{2,1,0:T(8,128)S(1)} %get-tuple-element.21), channel_id=1, source_target_pairs={{8,16},{16,8},{9,17},{17,9},{10,18},{18,10},{11,19},{19,11},{12,20... | collective-permute-start | bytes 1769480 | tf_op jit(solution)/shard_map/ppermute | solution.py:26
  41.0 11.4 %copy-start.2 = (f32[2,128,128]{2,1,0:T(8,128)S(1)}, f32[2,128,128]{2,1,0:T(8,128)}, u32[]{:S(2)}) copy-start(f32[2,128,128]{2,1,0:T(8,128)} %field_ref.1) | copy-start | bytes 393220
  41.7 10.7 %collective-permute-start.6 = (f32[3,128,128]{2,1,0:T(8,128)S(1)}, f32[3,128,128]{2,1,0:T(8,128)S(1)}, u32[]{:S(2)}, u32[]{:S(2)}) collective-permute-start(f32[3,128,128]{2,1,0:T(8,128)S(1)} %get-tuple-element.23), channel_id=1, source_target_pairs={{0,1},{1,0},{2,3},{3,2},{4,5},{5,4},{6,7},{7,6},{8,9},{9,8},{10,11... | collective-permute-start | bytes 589832 | tf_op jit(solution)/shard_map/ppermute | solution.py:26
  43.3 9.1 %collective-permute-start.7 = (f32[3,128,128]{2,1,0:T(8,128)S(1)}, f32[3,128,128]{2,1,0:T(8,128)S(1)}, u32[]{:S(2)}, u32[]{:S(2)}) collective-permute-start(f32[3,128,128]{2,1,0:T(8,128)S(1)} %get-tuple-element.24), channel_id=1, source_target_pairs={{1,2},{2,1},{3,4},{4,3},{5,6},{6,5},{9,10},{10,9},{11,12},{12,11},... | collective-permute-start | bytes 589832 | tf_op jit(solution)/shard_map/ppermute | solution.py:26
  52.4 7.8 %collective-permute-start.9 = (f32[2,128,128]{2,1,0:T(8,128)S(1)}, f32[2,128,128]{2,1,0:T(8,128)S(1)}, u32[]{:S(2)}, u32[]{:S(2)}) collective-permute-start(f32[2,128,128]{2,1,0:T(8,128)S(1)} %get-tuple-element.25.own_ref.field_ref), channel_id=1, source_target_pairs={{1,2},{2,1},{3,4},{4,3},{5,6},{6,5},{9,10},{10,9},{11,12},{12,11},... | collective-permute-start | bytes 393224 | tf_op jit(solution)/shard_map/ppermute | solution.py:26
  55.7 5.8 %collective-permute-start.8 = (f32[2,128,128]{2,1,0:T(8,128)S(1)}, f32[2,128,128]{2,1,0:T(8,128)S(1)}, u32[]{:S(2)}, u32[]{:S(2)}) collective-permute-start(f32[2,128,128]{2,1,0:T(8,128)S(1)} %get-tuple-element.25.own_ref.field_ref), channel_id=1, source_target_pairs={{0,1},{1,0},{2,3},{3,2},{4,5},{5,4},{6,7},{7,6},{8,9},{9,8},{10,11... | collective-permute-start | bytes 393224 | tf_op jit(solution)/shard_map/ppermute | solution.py:26
  62.1 9.1 %collective-permute-start.11 = (f32[2,128,384]{2,1,0:T(8,128)S(1)}, f32[2,128,384]{2,1,0:T(8,128)S(1)}, u32[]{:S(2)}, u32[]{:S(2)}) collective-permute-start(f32[2,128,384]{2,1,0:T(8,128)S(1)} %shard_map.69.strip_ref), channel_id=1, source_target_pairs={{8,16},{16,8},{9,17},{17,9},{10,18},{18,10},{11,19},{19,11},{12,20... | collective-permute-start | bytes 1179656 | tf_op jit(solution)/shard_map/ppermute | solution.py:26
  64.2 7.0 %collective-permute-start.10 = (f32[2,128,384]{2,1,0:T(8,128)S(1)}, f32[2,128,384]{2,1,0:T(8,128)S(1)}, u32[]{:S(2)}, u32[]{:S(2)}) collective-permute-start(f32[2,128,384]{2,1,0:T(8,128)S(1)} %shard_map.69.strip_ref), channel_id=1, source_target_pairs={{0,8},{8,0},{16,24},{24,16},{1,9},{9,1},{17,25},{25,17},{2,10},{10... | collective-permute-start | bytes 1179656 | tf_op jit(solution)/shard_map/ppermute | solution.py:26
  79.1 2.0 %collective-permute-start.12 = (f32[2,128,384]{2,1,0:T(8,128)S(1)}, f32[2,128,384]{2,1,0:T(8,128)S(1)}, u32[]{:S(2)}, u32[]{:S(2)}) collective-permute-start(f32[2,128,384]{2,1,0:T(8,128)S(1)} %get-tuple-element.28), channel_id=1, source_target_pairs={{0,8},{8,0},{16,24},{24,16},{1,9},{9,1},{17,25},{25,17},{2,10},{10... | collective-permute-start | bytes 1179656 | tf_op jit(solution)/shard_map/ppermute | solution.py:26
  79.2 9.1 %collective-permute-start.13 = (f32[2,128,384]{2,1,0:T(8,128)S(1)}, f32[2,128,384]{2,1,0:T(8,128)S(1)}, u32[]{:S(2)}, u32[]{:S(2)}) collective-permute-start(f32[2,128,384]{2,1,0:T(8,128)S(1)} %get-tuple-element.29), channel_id=1, source_target_pairs={{8,16},{16,8},{9,17},{17,9},{10,18},{18,10},{11,19},{19,11},{12,20... | collective-permute-start | bytes 1179656 | tf_op jit(solution)/shard_map/ppermute | solution.py:26
  88.9 5.0 %collective-permute-start.14 = (f32[2,128,128]{2,1,0:T(8,128)S(1)}, f32[2,128,128]{2,1,0:T(8,128)S(1)}, u32[]{:S(2)}, u32[]{:S(2)}) collective-permute-start(f32[2,128,128]{2,1,0:T(8,128)S(1)} %get-tuple-element.31), channel_id=1, source_target_pairs={{0,1},{1,0},{2,3},{3,2},{4,5},{5,4},{6,7},{7,6},{8,9},{9,8},{10,11... | collective-permute-start | bytes 393224 | tf_op jit(solution)/shard_map/ppermute | solution.py:26
  90.5 7.7 %collective-permute-start.15 = (f32[2,128,128]{2,1,0:T(8,128)S(1)}, f32[2,128,128]{2,1,0:T(8,128)S(1)}, u32[]{:S(2)}, u32[]{:S(2)}) collective-permute-start(f32[2,128,128]{2,1,0:T(8,128)S(1)} %get-tuple-element.32), channel_id=1, source_target_pairs={{1,2},{2,1},{3,4},{4,3},{5,6},{6,5},{9,10},{10,9},{11,12},{12,11},... | collective-permute-start | bytes 393224 | tf_op jit(solution)/shard_map/ppermute | solution.py:26
where the time goes:
time: 99.3 us; the launch traced here: 99 us
  waiting for transfers between devices  50 us (50%)
  starting transfers between devices  25.9 us (26%)
  Pallas kernels  20.4 us (21%)
  local copies, waits for them, and re-layouts  2.33 us (2%)
    ppermute x16, waiting for transfers between devices, swap(): return lax.ppermute(value, axis, pairs)  50 us
    ppermute x16, starting transfers between devices, swap(): return lax.ppermute(value, axis, pairs)  25.9 us
    pallas_call x9, Pallas kernels, call(): pl.pallas_call(kernel, out_shape=outs, in_specs=specs, out_specs=[VMEM] *...  20.4 us
    unnamed x15, local copies, waits for them, and re-layouts  2.24 us
  transfers between devices with their start and end apart: 16, of which 11 were waited for; matrix products, arithmetic and copies ran while one was open for 0% of the time, Pallas kernels for 1%

commit v1 on v0

--- a/solution.py
+++ b/solution.py
@@ -1,4 +1,3 @@
-import functools
 import math
 
 import jax
@@ -9,6 +8,7 @@
 from jax.experimental.pallas import tpu as pltpu
 from jax.sharding import PartitionSpec as P
 
+
 ITERS = 2
 FLOOR = 0.5
 f32 = jnp.float32
@@ -17,13 +17,33 @@
 SMEM = pl.BlockSpec(memory_space=pltpu.SMEM)
 
 
-def swap(value, axis, odd):
-    n = lax.axis_size(axis)
-    first = 1 if odd else 0
+def mate(i, n, odd):
+    other = ((i + 1) ^ 1) - 1 if odd else i ^ 1
+    return other if 0 <= other < n else None
+
+
+def swap(value, row=None, col=None):
+    rows, cols = lax.axis_size("rows"), lax.axis_size("cols")
+    far = 2 if cols % 4 == 0 else 1
     pairs = []
-    for i in range(first, n - 1, 2):
-        pairs += [(i, i + 1), (i + 1, i)]
-    return lax.ppermute(value, axis, pairs)
+    for r in range(rows):
+        for c in range(cols):
+            to_r = r if row is None else mate(r, rows, row)
+            to_c = c if col is None else mate(c, cols, col)
+            if to_r is None:
+                to_r, to_c = r, c ^ far
+            elif to_c is None:
+                to_r, to_c = (r ^ 1 if row is None else to_r), c
+            pairs.append((r * cols + c, to_r * cols + to_c))
+    return lax.ppermute(value, ("rows", "cols"), pairs)
+
+
+def halo(tile):
+    col_odd = swap(tile, col=1)
+    col_even = swap(tile, col=0)
+    odd_row = [swap(tile, row=1), swap(tile, row=1, col=0), swap(tile, row=1, col=1)]
+    even_row = [swap(tile, row=0), swap(col_even, row=0), swap(col_odd, row=0)]
+    return [tile, col_even, col_odd] + even_row + odd_row
 
 
 def dft_matrices(size):
@@ -95,26 +115,36 @@
     return pltpu.roll(wide, shift, 1)
 
 
-def windows_kernel(
-    with_light, flags_ref, offs_ref, strip_ref, even_ref, odd_ref, probe_ref, amps_ref,
-    mats_ref, mid_ref, to_even_ref, to_odd_ref, ext, acc,
-):
-    own = strip_ref.shape[1]
+def is_there(flags_ref, g, m):
+    if g == 2:
+        both = flags_ref[2] * flags_ref[3] if m == 2 else flags_ref[2]
+        return both > 0
+    return flags_ref[3] > 0 if m == 2 else None
+
+
+def windows_kernel(flags_ref, offs_ref, *refs):
+    tiles = refs[:9]
+    probe_ref, amps_ref, mats, mid_ref, to_even_ref, ro_ref, de_ref, do_ref, ext, acc = refs[9:]
+    own = mid_ref.shape[1]
     extent = 3 * own
     size = probe_ref.shape[1]
     half = size // 2
     positions = amps_ref.shape[0]
-    parity = flags_ref[0]
-    even_at = pl.multiple_of((1 - parity) * 2 * own, own)
-    odd_at = pl.multiple_of(parity * 2 * own, own)
-    for k in range(2):
-        for j in range(3):
-            lanes = slice(j * own, (j + 1) * own)
-            ext[3 * k + j, own : 2 * own, :] = strip_ref[k, :, lanes]
-            ext[3 * k + j, pl.ds(even_at, own), :] = even_ref[k, :, lanes]
-            ext[3 * k + j, pl.ds(odd_at, own), :] = odd_ref[k, :, lanes]
+    row_parity = flags_ref[0]
+    col_parity = flags_ref[1]
+    even_at = pl.multiple_of((1 - row_parity) * 2 * own, own)
+    odd_at = pl.multiple_of(row_parity * 2 * own, own)
+    even_chunk = 2 * (1 - col_parity)
+    odd_chunk = 2 * col_parity
+    for g, at in enumerate((own, even_at, odd_at)):
+        for m, chunk in enumerate((1, even_chunk, odd_chunk)):
+            there = is_there(flags_ref, g, m)
+            for k in range(2):
+                tile = tiles[3 * g + m][k * own : (k + 1) * own, :]
+                if there is not None:
+                    tile = jnp.where(there, tile, 0.0)
+                ext[3 * k + chunk, pl.ds(at, own), :] = tile
     acc[...] = jnp.zeros_like(acc)
-    mats = mats_ref
 
     def window_of(k, rows, back_by):
         wide = jnp.concatenate([ext[3 * k + j, rows, :] for j in range(3)], 1)
@@ -175,8 +205,6 @@
             rows = pl.ds(first + h * half, half)
             add_at(0, rows, pr * br + pi * bi, second)
             add_at(1, rows, pr * bi - pi * br, second)
-            if with_light:
-                add_at(2, rows, pr * pr + pi * pi, second)
 
     for p in range(positions):
         window(p)
@@ -185,55 +213,79 @@
             lanes = slice(j * own, (j + 1) * own)
             mid_ref[k, :, lanes] = acc[3 * k + j, own : 2 * own, :]
             to_even_ref[k, :, lanes] = acc[3 * k + j, pl.ds(even_at, own), :]
-            to_odd_ref[k, :, lanes] = acc[3 * k + j, pl.ds(odd_at, own), :]
-
-
-def join_kernel(flags_ref, own_ref, even_ref, odd_ref, strip_ref):
-    own = own_ref.shape[2]
-    parity = flags_ref[1]
-    strip_ref[:, :, own : 2 * own] = own_ref[...]
-
-    @pl.when(parity == 0)
-    def _():
-        strip_ref[:, :, 2 * own :] = even_ref[...]
-        strip_ref[:, :, :own] = odd_ref[...]
-
-    @pl.when(parity == 1)
-    def _():
-        strip_ref[:, :, 2 * own :] = odd_ref[...]
-        strip_ref[:, :, :own] = even_ref[...]
-
-
-def rows_kernel(flags_ref, mid_ref, even_ref, odd_ref, keep_ref, to_even_ref, to_odd_ref):
-    own = keep_ref.shape[2]
-    parity = flags_ref[1]
-    total = mid_ref[...] + even_ref[...] + odd_ref[...]
-    keep_ref[...] = total[:, :, own : 2 * own]
-
-    @pl.when(parity == 0)
-    def _():
-        to_even_ref[...] = total[:, :, 2 * own :]
-        to_odd_ref[...] = total[:, :, :own]
-
-    @pl.when(parity == 1)
-    def _():
-        to_even_ref[...] = total[:, :, :own]
-        to_odd_ref[...] = total[:, :, 2 * own :]
-
-
-def first_update_kernel(field_ref, keep_ref, even_ref, odd_ref, out_ref, light_ref):
-    total = keep_ref[...] + even_ref[...] + odd_ref[...]
-    light = total[2] + 1.0
-    light_ref[...] = light
-    out_ref[0] = field_ref[0] - total[0] / light
-    out_ref[1] = field_ref[1] - total[1] / light
-
-
-def update_kernel(field_ref, light_ref, keep_ref, even_ref, odd_ref, out_ref):
-    total = keep_ref[...] + even_ref[...] + odd_ref[...]
+        rows = slice(k * own, (k + 1) * own)
+        for out, chunk in ((ro_ref, 1), (de_ref, even_chunk), (do_ref, odd_chunk)):
+            out[rows, :] = acc[3 * k + chunk, pl.ds(odd_at, own), :]
+
+
+def pack_kernel(offs_ref, field_ref, out_ref):
+    own = field_ref.shape[1]
+    for k in range(2):
+        out_ref[k * own : (k + 1) * own, :] = field_ref[k]
+    lanes = lax.broadcasted_iota(jnp.int32, (8, own), 1)
+    row = jnp.zeros((8, own), jnp.int32)
+    for j in range(offs_ref.shape[0]):
+        row = jnp.where(lanes == j, offs_ref[j], row)
+    out_ref[2 * own :, :] = row.astype(f32)
+
+
+def light_kernel(flags_ref, offs_ref, probe_ref, light_ref, padded):
+    own = light_ref.shape[0]
+    size = probe_ref.shape[1]
+    positions = offs_ref.shape[0] // 18
+    padded[...] = jnp.zeros_like(padded)
+    power = probe_ref[0] * probe_ref[0] + probe_ref[1] * probe_ref[1]
+    for j in range(size // own):
+        padded[1 + j, own : own + size, :] = power[:, j * own : (j + 1) * own]
+    light_ref[...] = jnp.ones_like(light_ref)
+    lanes = lax.broadcasted_iota(jnp.int32, (own, own), 1)
+    row_step = (1 - 2 * flags_ref[0]) * own
+    col_step = (1 - 2 * flags_ref[1]) * own
+    for g, row in enumerate((0, row_step, -row_step)):
+        for m, col in enumerate((0, col_step, -col_step)):
+            for p in range(positions):
+                at = 2 * ((3 * g + m) * positions + p)
+                first = 2 * own - row - offs_ref[at]
+                second = 2 * own - col - offs_ref[at + 1]
+
+                there = is_there(flags_ref, g, m)
+
+                @pl.when(True if there is None else there)
+                def _():
+                    chunk = second // own
+                    by = second - chunk * own
+                    back = jnp.where(by == 0, 0, own - by)
+                    rows = pl.ds(first, own)
+                    left = pltpu.roll(padded[chunk, rows, :], back, 1)
+                    right = pltpu.roll(padded[chunk + 1, rows, :], back, 1)
+                    light_ref[...] += jnp.where(lanes < own - by, left, right)
+
+
+def rows_kernel(flags_ref, mid_ref, even_ref, keep_ref, to_even_ref, to_odd_ref):
+    own = keep_ref.shape[1]
+    col_parity = flags_ref[1]
+    for k in range(2):
+        rows = slice(k * own, (k + 1) * own)
+        total = mid_ref[k] + even_ref[k]
+        left, right = total[:, :own], total[:, 2 * own :]
+        keep_ref[rows, :] = total[:, own : 2 * own]
+        to_even_ref[rows, :] = jnp.where(col_parity == 0, right, left)
+        to_odd_ref[rows, :] = jnp.where(col_parity == 0, left, right)
+
+
+def update_kernel(
+    flags_ref, field_ref, light_ref, keep_ref, ce_ref, co_ref, ro_ref, de_ref, do_ref, out_ref
+):
+    own = light_ref.shape[0]
+    row_ok, col_ok = flags_ref[2] > 0, flags_ref[3] > 0
     light = light_ref[...]
-    out_ref[0] = field_ref[0] - total[0] / light
-    out_ref[1] = field_ref[1] - total[1] / light
+    for k in range(2):
+        rows = slice(k * own, (k + 1) * own)
+        total = keep_ref[rows, :] + ce_ref[rows, :]
+        total += jnp.where(col_ok, co_ref[rows, :], 0.0)
+        odd_row = ro_ref[rows, :] + de_ref[rows, :] + jnp.where(col_ok, do_ref[rows, :], 0.0)
+        total += jnp.where(row_ok, odd_row, 0.0)
+        out_ref[rows, :] = field_ref[rows, :] - total / light
 
 
 def call(kernel, shapes, specs, *args, scratch=(), flops=0):
@@ -258,7 +310,11 @@
     extent = 3 * own
     amps = amplitudes.reshape(positions, size, size)
     offs = offsets.reshape(2 * positions)
-    flags = jnp.stack([lax.axis_index("rows") % 2, lax.axis_index("cols") % 2]).astype(jnp.int32)
+    row, col = lax.axis_index("rows"), lax.axis_index("cols")
+    inner = [
+        (at > 0) & (at < lax.axis_size(axis) - 1) for axis, at in (("rows", row), ("cols", col))
+    ]
+    flags = jnp.stack([row % 2, col % 2] + [x.astype(row.dtype) for x in inner]).astype(jnp.int32)
     mats = jnp.asarray(dft_matrices(size))
     order = np.concatenate([np.arange(0, size, 2), np.arange(1, size, 2)])
     perm = (np.arange(size)[:, None] == order[None, :]).astype(jnp.bfloat16)
@@ -267,38 +323,38 @@
         amps_kernel, [(positions, size, size)], [VMEM, VMEM], amps, perm,
         flops=6 * positions * size**3,
     )
-    field = object_field
-    light = None
+    field = call(
+        pack_kernel, [(2 * own + 8, own)], [SMEM, VMEM], offs, object_field
+    )
+    tiles = halo(field)
+    around = jnp.concatenate([t[2 * own, : 2 * positions] for t in tiles]).astype(jnp.int32)
+    light = call(
+        light_kernel, [(own, own)], [SMEM, SMEM, VMEM], flags, around, probe,
+        scratch=[pltpu.VMEM((2 + size // own + 1, size + 2 * own, own), f32)],
+        flops=4 * positions * size**3,
+    )
     for step in range(ITERS):
-        layers = 3 if step == 0 else 2
-        strip = call(
-            join_kernel, [(2, own, extent)], [SMEM] + [VMEM] * 3,
-            flags, field, swap(field, "cols", False), swap(field, "cols", True),
-        )
-        mid, to_even, to_odd = call(
-            functools.partial(windows_kernel, step == 0),
-            [(layers, own, extent)] * 3,
-            [SMEM, SMEM] + [VMEM] * 6,
-            flags, offs, strip, swap(strip, "rows", False), swap(strip, "rows", True),
-            probe, amps, mats,
-            scratch=[pltpu.VMEM((3 * k, extent, own), f32) for k in (2, layers)],
+        if step > 0:
+            tiles = halo(field)
+        mid, to_even, ro, de, do = call(
+            windows_kernel,
+            [(2, own, extent)] * 2 + [(2 * own, own)] * 3,
+            [SMEM, SMEM] + [VMEM] * 12,
+            flags, offs, *tiles, probe, amps, mats,
+            scratch=[pltpu.VMEM((6, extent, own), f32)] * 2,
             flops=48 * positions * size**3,
         )
+        even = swap(to_even, row=0)
+        odd_row = [swap(ro, row=1), swap(de, row=1, col=0), swap(do, row=1, col=1)]
         keep, to_even, to_odd = call(
-            rows_kernel, [(layers, own, own)] * 3, [SMEM] + [VMEM] * 3,
-            flags, mid, swap(to_even, "rows", False), swap(to_odd, "rows", True),
-        )
-        even, odd = swap(to_even, "cols", False), swap(to_odd, "cols", True)
-        if step == 0:
-            field, light = call(
-                first_update_kernel, [(2, own, own), (own, own)], [VMEM] * 4,
-                field, keep, even, odd,
-            )
-        else:
-            field = call(
-                update_kernel, [(2, own, own)], [VMEM] * 5, field, light, keep, even, odd
-            )
-    return field
+            rows_kernel, [(2 * own, own)] * 3, [SMEM] + [VMEM] * 2, flags, mid, even
+        )
+        co, ce = swap(to_odd, col=1), swap(to_even, col=0)
+        field = call(
+            update_kernel, [(2 * own, own)], [SMEM] + [VMEM] * 8,
+            flags, field, light, keep, ce, co, *odd_row,
+        )
+    return field.reshape(2, own, own)
 
 
 def solution(mesh):
@@ -308,6 +364,7 @@
         P("rows", "cols", None, None, None),
         P("rows", "cols", None, None),
     )
+
     return jax.shard_map(
         local, mesh=mesh, in_specs=placed, out_specs=P(None, "rows", "cols"), check_vma=False
     )

time: 99.3 us -> 80.4 us (0.81); the launches traced: 99 us -> 78.8 us
  waiting for transfers between devices: 50 us -> 24.7 us
  Pallas kernels: 20.4 us -> 24.4 us
    ppermute x16 -> x28, waiting for transfers between devices: 50 us -> 24.7 us  [swap(): return lax.ppermute(value, ('rows', 'cols'), pairs)]
    pallas_call x9, Pallas kernels: 20.4 us -> 24.4 us  [call(): pl.pallas_call(kernel, out_shape=outs, in_specs=specs, out_specs=[VMEM] *...]
    unnamed x15 -> x13, local copies, waits for them, and re-layouts: 2.24 us -> 2.95 us
    ppermute x16 -> x28, starting transfers between devices: 25.9 us -> 26.3 us  [swap(): return lax.ppermute(value, ('rows', 'cols'), pairs)]
  transfers between devices with their start and end apart: 16 -> 28, of which waited for: 11 -> 10; matrix products, arithmetic and copies ran while one was open for 0% -> 0% of each run, Pallas kernels for 1% -> 8%
where the time goes in v1:
time: 80.4 us; the launch traced here: 78.8 us
  starting transfers between devices  26.3 us (33%)
  waiting for transfers between devices  24.7 us (31%)
  Pallas kernels  24.4 us (30%)
  local copies, waits for them, and re-layouts  3.14 us (4%)
    ppermute x28, starting transfers between devices, swap(): return lax.ppermute(value, ('rows', 'cols'), pairs)  26.3 us
    ppermute x28, waiting for transfers between devices, swap(): return lax.ppermute(value, ('rows', 'cols'), pairs)  24.7 us
    pallas_call x9, Pallas kernels, call(): pl.pallas_call(kernel, out_shape=outs, in_specs=specs, out_specs=[VMEM] *...  24.4 us
    unnamed x13, local copies, waits for them, and re-layouts  2.95 us
  transfers between devices with their start and end apart: 28, of which 10 were waited for; matrix products, arithmetic and copies ran while one was open for 0% of the time, Pallas kernels for 8%

profile of v1, /device:TPU:20, one launch (start us, length us, event | category | flops | bytes accessed | tf_op | source)
XLA Modules:
  0.0 78.8 jit_solution(14882055657916498950)
XLA Ops:
  3.2 2.9 %collective-permute-start.6 = (f32[264,128]{1,0:T(8,128)S(1)}, f32[264,128]{1,0:T(8,128)S(1)}, u32[]{:S(2)}, u32[]{:S(2)}) collective-permute-start(f32[264,128]{1,0:T(8,128)S(1)} %shard_map.64.refs_0_.field_ref), channel_id=1, source_target_pairs={{0,2},{1,3},{2,0},{3,1},{4,6},{5,7},{6,4},{7,5},{8,17},{9,16},{10,... | collective-permute-start | bytes 405512 | tf_op jit(solution)/shard_map/ppermute | solution.py:38
  7.8 1.3 %shard_map.66.refs_10_ = f32[4,256,256]{2,1,0:T(8,128)S(1)} custom-call(f32[4,256,256]{2,1,0:T(8,128)S(1)} %bitcast.24, bf16[2,256,256]{2,1,0:T(8,128)(2,1)S(1)} %copy-done.1), custom_call_target="tpu_custom_call" | custom-call | flops 402653184 | bytes 1310720 | tf_op jit(solution)/shard_map/pallas_call | solution.py:294
  9.2 3.8 %collective-permute-done.1.refs_2_ = f32[264,128]{1,0:T(8,128)S(1)} collective-permute-done((f32[264,128]{1,0:T(8,128)S(1)}, f32[264,128]{1,0:T(8,128)S(1)}, u32[]{:S(2)}, u32[]{:S(2)}) %collective-permute-start.1) | collective-permute-done | bytes 135200 | tf_op jit(solution)/shard_map/ppermute | solution.py:38
  14.6 4.0 %collective-permute-done.refs_1_ = f32[264,128]{1,0:T(8,128)S(1)} collective-permute-done((f32[264,128]{1,0:T(8,128)S(1)}, f32[264,128]{1,0:T(8,128)S(1)}, u32[]{:S(2)}, u32[]{:S(2)}) %collective-permute-start) | collective-permute-done | bytes 135200 | tf_op jit(solution)/shard_map/ppermute | solution.py:38
  18.7 1.3 %collective-permute-done.3.refs_4_ = f32[264,128]{1,0:T(8,128)S(1)} collective-permute-done((f32[264,128]{1,0:T(8,128)S(1)}, f32[264,128]{1,0:T(8,128)S(1)}, u32[]{:S(2)}, u32[]{:S(2)}) %collective-permute-start.3) | collective-permute-done | bytes 135200 | tf_op jit(solution)/shard_map/ppermute | solution.py:38
  19.9 8.0 %shard_map.67 = (f32[2,128,384]{2,1,0:T(8,128)S(1)}, f32[2,128,384]{2,1,0:T(8,128)S(1)}, f32[256,128]{1,0:T(8,128)S(1)}, f32[256,128]{1,0:T(8,128)S(1)}, f32[256,128]{1,0:T(8,128)S(1)}) custom-call(s32[4]{0:T(128)S(1)} %pad_add_fusion.flags_ref, s32[8]{0:T(128)S(1)} %reshape.9.offs_ref, f32[264,128]{1,0:T(8,128)S(1)} %shard_map.64.refs_0_.field_ref, ...), custom_call_target="tpu_custom_call" | custom-call | flops 3221225472 | bytes 3838000 | tf_op jit(solution)/shard_map/pallas_call | solution.py:294
  29.2 1.9 %collective-permute-start.12 = (f32[256,128]{1,0:T(8,128)S(1)}, f32[256,128]{1,0:T(8,128)S(1)}, u32[]{:S(2)}, u32[]{:S(2)}) collective-permute-start(f32[256,128]{1,0:T(8,128)S(1)} %get-tuple-element.27), channel_id=1, source_target_pairs={{0,2},{1,3},{2,0},{3,1},{4,6},{5,7},{6,4},{7,5},{8,17},{9,16},{10,... | collective-permute-start | bytes 393224 | tf_op jit(solution)/shard_map/ppermute | solution.py:38
  31.1 2.1 %collective-permute-start.13 = (f32[256,128]{1,0:T(8,128)S(1)}, f32[256,128]{1,0:T(8,128)S(1)}, u32[]{:S(2)}, u32[]{:S(2)}) collective-permute-start(f32[256,128]{1,0:T(8,128)S(1)} %get-tuple-element.28), channel_id=1, source_target_pairs={{0,2},{1,3},{2,0},{3,1},{4,6},{5,7},{6,4},{7,5},{8,16},{9,18},{10,... | collective-permute-start | bytes 393224 | tf_op jit(solution)/shard_map/ppermute | solution.py:38
  35.6 3.7 %shard_map.65.light_ref = f32[128,128]{1,0:T(8,128)S(1)} custom-call(s32[4]{0:T(128)S(1)} %pad_add_fusion.flags_ref, s32[72]{0:T(128)S(1)} %convert_element_type.2.offs_ref, f32[2,256,256]{2,1,0:T(8,128)S(1)} %copy-done.3), custom_call_target="tpu_custom_call" | custom-call | flops 268435456 | bytes 524592 | tf_op jit(solution)/shard_map/pallas_call | solution.py:294
  39.3 2.1 %collective-permute-done.9.ce_ref = f32[256,128]{1,0:T(8,128)S(1)} collective-permute-done((f32[256,128]{1,0:T(8,128)S(1)}, f32[256,128]{1,0:T(8,128)S(1)}, u32[]{:S(2)}, u32[]{:S(2)}) %collective-permute-start.9) | collective-permute-done | bytes 131104 | tf_op jit(solution)/shard_map/ppermute | solution.py:38
  42.0 2.1 %collective-permute-start.21 = (f32[256,128]{1,0:T(8,128)S(1)}, f32[256,128]{1,0:T(8,128)S(1)}, u32[]{:S(2)}, u32[]{:S(2)}) collective-permute-start(f32[256,128]{1,0:T(8,128)S(1)} %shard_map.69.refs_0_.field_ref), channel_id=1, source_target_pairs={{0,2},{1,3},{2,0},{3,1},{4,6},{5,7},{6,4},{7,5},{8,16},{9,18},{10,... | collective-permute-start | bytes 393224 | tf_op jit(solution)/shard_map/ppermute | solution.py:38
  44.2 1.3 %collective-permute-start.15 = (f32[256,128]{1,0:T(8,128)S(1)}, f32[256,128]{1,0:T(8,128)S(1)}, u32[]{:S(2)}, u32[]{:S(2)}) collective-permute-start(f32[256,128]{1,0:T(8,128)S(1)} %shard_map.69.refs_0_.field_ref), channel_id=1, source_target_pairs={{0,8},{1,2},{2,1},{3,4},{4,3},{5,6},{6,5},{7,15},{8,0},{9,10},{10,... | collective-permute-start | bytes 393224 | tf_op jit(solution)/shard_map/ppermute | solution.py:38
  45.5 1.6 %collective-permute-start.14 = (f32[256,128]{1,0:T(8,128)S(1)}, f32[256,128]{1,0:T(8,128)S(1)}, u32[]{:S(2)}, u32[]{:S(2)}) collective-permute-start(f32[256,128]{1,0:T(8,128)S(1)} %shard_map.69.refs_0_.field_ref), channel_id=1, source_target_pairs={{0,1},{1,0},{2,3},{3,2},{4,5},{5,4},{6,7},{7,6},{8,9},{9,8},{10,11... | collective-permute-start | bytes 393224 | tf_op jit(solution)/shard_map/ppermute | solution.py:38
  47.1 1.6 %collective-permute-start.19 = (f32[256,128]{1,0:T(8,128)S(1)}, f32[256,128]{1,0:T(8,128)S(1)}, u32[]{:S(2)}, u32[]{:S(2)}) collective-permute-start(f32[256,128]{1,0:T(8,128)S(1)} %shard_map.69.refs_0_.field_ref), channel_id=1, source_target_pairs={{0,2},{1,3},{2,0},{3,1},{4,6},{5,7},{6,4},{7,5},{8,16},{9,17},{10,... | collective-permute-start | bytes 393224 | tf_op jit(solution)/shard_map/ppermute | solution.py:38
  48.7 1.5 %collective-permute-done.15.refs_2_ = f32[256,128]{1,0:T(8,128)S(1)} collective-permute-done((f32[256,128]{1,0:T(8,128)S(1)}, f32[256,128]{1,0:T(8,128)S(1)}, u32[]{:S(2)}, u32[]{:S(2)}) %collective-permute-start.15) | collective-permute-done | bytes 131104 | tf_op jit(solution)/shard_map/ppermute | solution.py:38
  50.1 1.3 %collective-permute-done.14.refs_1_ = f32[256,128]{1,0:T(8,128)S(1)} collective-permute-done((f32[256,128]{1,0:T(8,128)S(1)}, f32[256,128]{1,0:T(8,128)S(1)}, u32[]{:S(2)}, u32[]{:S(2)}) %collective-permute-start.14) | collective-permute-done | bytes 131104 | tf_op jit(solution)/shard_map/ppermute | solution.py:38
  51.4 3.9 %collective-permute-done.20.refs_7_ = f32[256,128]{1,0:T(8,128)S(1)} collective-permute-done((f32[256,128]{1,0:T(8,128)S(1)}, f32[256,128]{1,0:T(8,128)S(1)}, u32[]{:S(2)}, u32[]{:S(2)}) %collective-permute-start.20) | collective-permute-done | bytes 131104 | tf_op jit(solution)/shard_map/ppermute | solution.py:38
  55.3 7.8 %shard_map.70 = (f32[2,128,384]{2,1,0:T(8,128)S(1)}, f32[2,128,384]{2,1,0:T(8,128)S(1)}, f32[256,128]{1,0:T(8,128)S(1)}, f32[256,128]{1,0:T(8,128)S(1)}, f32[256,128]{1,0:T(8,128)S(1)}) custom-call(s32[4]{0:T(128)S(1)} %pad_add_fusion.flags_ref, s32[8]{0:T(128)S(1)} %reshape.9.offs_ref, f32[256,128]{1,0:T(8,128)S(1)} %shard_map.69.refs_0_.field_ref, ...), custom_call_target="tpu_custom_call" | custom-call | flops 3221225472 | bytes 3801136 | tf_op jit(solution)/shard_map/pallas_call | solution.py:294
  64.2 2.7 %collective-permute-start.26 = (f32[256,128]{1,0:T(8,128)S(1)}, f32[256,128]{1,0:T(8,128)S(1)}, u32[]{:S(2)}, u32[]{:S(2)}) collective-permute-start(f32[256,128]{1,0:T(8,128)S(1)} %get-tuple-element.35), channel_id=1, source_target_pairs={{0,2},{1,3},{2,0},{3,1},{4,6},{5,7},{6,4},{7,5},{8,17},{9,16},{10,... | collective-permute-start | bytes 393224 | tf_op jit(solution)/shard_map/ppermute | solution.py:38
  66.8 1.5 %collective-permute-start.27 = (f32[256,128]{1,0:T(8,128)S(1)}, f32[256,128]{1,0:T(8,128)S(1)}, u32[]{:S(2)}, u32[]{:S(2)}) collective-permute-start(f32[256,128]{1,0:T(8,128)S(1)} %get-tuple-element.36), channel_id=1, source_target_pairs={{0,2},{1,3},{2,0},{3,1},{4,6},{5,7},{6,4},{7,5},{8,16},{9,18},{10,... | collective-permute-start | bytes 393224 | tf_op jit(solution)/shard_map/ppermute | solution.py:38
  69.1 1.7 %collective-permute-start.24 = (f32[256,128]{1,0:T(8,128)S(1)}, f32[256,128]{1,0:T(8,128)S(1)}, u32[]{:S(2)}, u32[]{:S(2)}) collective-permute-start(f32[256,128]{1,0:T(8,128)S(1)} %get-tuple-element.33), channel_id=1, source_target_pairs={{0,8},{1,2},{2,1},{3,4},{4,3},{5,6},{6,5},{7,15},{8,0},{9,10},{10,... | collective-permute-start | bytes 393224 | tf_op jit(solution)/shard_map/ppermute | solution.py:38
  71.3 1.9 %collective-permute-done.27.do_ref = f32[256,128]{1,0:T(8,128)S(1)} collective-permute-done((f32[256,128]{1,0:T(8,128)S(1)}, f32[256,128]{1,0:T(8,128)S(1)}, u32[]{:S(2)}, u32[]{:S(2)}) %collective-permute-start.27) | collective-permute-done | bytes 131104 | tf_op jit(solution)/shard_map/ppermute | solution.py:38
  73.1 4.4 %collective-permute-done.23.ce_ref = f32[256,128]{1,0:T(8,128)S(1)} collective-permute-done((f32[256,128]{1,0:T(8,128)S(1)}, f32[256,128]{1,0:T(8,128)S(1)}, u32[]{:S(2)}, u32[]{:S(2)}) %collective-permute-start.23) | collective-permute-done | bytes 131104 | tf_op jit(solution)/shard_map/ppermute | solution.py:38
  77.5 1.3 %shard_map.72 = f32[256,128]{1,0:T(8,128)} custom-call(s32[4]{0:T(128)S(1)} %pad_add_fusion.flags_ref, f32[256,128]{1,0:T(8,128)S(1)} %shard_map.69.refs_0_.field_ref, f32[128,128]{1,0:T(8,128)S(1)} %shard_map.65.light_ref, f32[256,128]{1,0:T(8,128)S(1)} %get-tuple-element.31.keep_ref, f32[256,128]{1,0:T(8,128)S(1)} %collective-permute-done.23.ce_ref, ...), custom_call_target="tpu_custom_call" | custom-call | bytes 983056 | tf_op jit(solution)/shard_map/pallas_call | solution.py:294
  (67 shorter events, 13.0 us)
Async XLA Ops:
  2.4 11.7 %collective-permute-start.7 = (f32[264,128]{1,0:T(8,128)S(1)}, f32[264,128]{1,0:T(8,128)S(1)}, u32[]{:S(2)}, u32[]{:S(2)}) collective-permute-start(f32[264,128]{1,0:T(8,128)S(1)} %shard_map.64.refs_0_.field_ref), channel_id=1, source_target_pairs={{0,2},{1,3},{2,0},{3,1},{4,6},{5,7},{6,4},{7,5},{8,16},{9,18},{10,... | collective-permute-start | bytes 405512 | tf_op jit(solution)/shard_map/ppermute | solution.py:38
  3.2 15.4 %collective-permute-start.6 = (f32[264,128]{1,0:T(8,128)S(1)}, f32[264,128]{1,0:T(8,128)S(1)}, u32[]{:S(2)}, u32[]{:S(2)}) collective-permute-start(f32[264,128]{1,0:T(8,128)S(1)} %shard_map.64.refs_0_.field_ref), channel_id=1, source_target_pairs={{0,2},{1,3},{2,0},{3,1},{4,6},{5,7},{6,4},{7,5},{8,17},{9,16},{10,... | collective-permute-start | bytes 405512 | tf_op jit(solution)/shard_map/ppermute | solution.py:38
  6.1 12.5 %collective-permute-start.5 = (f32[264,128]{1,0:T(8,128)S(1)}, f32[264,128]{1,0:T(8,128)S(1)}, u32[]{:S(2)}, u32[]{:S(2)}) collective-permute-start(f32[264,128]{1,0:T(8,128)S(1)} %shard_map.64.refs_0_.field_ref), channel_id=1, source_target_pairs={{0,2},{1,3},{2,0},{3,1},{4,6},{5,7},{6,4},{7,5},{8,16},{9,17},{10,... | collective-permute-start | bytes 405512 | tf_op jit(solution)/shard_map/ppermute | solution.py:38
  6.1 12.5 %collective-permute-start.2 = (f32[264,128]{1,0:T(8,128)S(1)}, f32[264,128]{1,0:T(8,128)S(1)}, u32[]{:S(2)}, u32[]{:S(2)}) collective-permute-start(f32[264,128]{1,0:T(8,128)S(1)} %shard_map.64.refs_0_.field_ref), channel_id=1, source_target_pairs={{0,8},{1,9},{2,10},{3,11},{4,12},{5,13},{6,14},{7,15},{8,0},{9,1},... | collective-permute-start | bytes 405512 | tf_op jit(solution)/shard_map/ppermute | solution.py:38
  6.1 6.9 %collective-permute-start.1 = (f32[264,128]{1,0:T(8,128)S(1)}, f32[264,128]{1,0:T(8,128)S(1)}, u32[]{:S(2)}, u32[]{:S(2)}) collective-permute-start(f32[264,128]{1,0:T(8,128)S(1)} %shard_map.64.refs_0_.field_ref), channel_id=1, source_target_pairs={{0,8},{1,2},{2,1},{3,4},{4,3},{5,6},{6,5},{7,15},{8,0},{9,10},{10,... | collective-permute-start | bytes 405512 | tf_op jit(solution)/shard_map/ppermute | solution.py:38
  13.0 5.6 %collective-permute-start = (f32[264,128]{1,0:T(8,128)S(1)}, f32[264,128]{1,0:T(8,128)S(1)}, u32[]{:S(2)}, u32[]{:S(2)}) collective-permute-start(f32[264,128]{1,0:T(8,128)S(1)} %shard_map.64.refs_0_.field_ref), channel_id=1, source_target_pairs={{0,1},{1,0},{2,3},{3,2},{4,5},{5,4},{6,7},{7,6},{8,9},{9,8},{10,11... | collective-permute-start | bytes 405512 | tf_op jit(solution)/shard_map/ppermute | solution.py:38
  27.9 5.2 %collective-permute-start.8 = (f32[2,128,384]{2,1,0:T(8,128)S(1)}, f32[2,128,384]{2,1,0:T(8,128)S(1)}, u32[]{:S(2)}, u32[]{:S(2)}) collective-permute-start(f32[2,128,384]{2,1,0:T(8,128)S(1)} %get-tuple-element.22), channel_id=1, source_target_pairs={{0,8},{1,9},{2,10},{3,11},{4,12},{5,13},{6,14},{7,15},{8,0},{9,1},... | collective-permute-start | bytes 1179656 | tf_op jit(solution)/shard_map/ppermute | solution.py:38
  28.1 11.1 %collective-permute-start.11 = (f32[256,128]{1,0:T(8,128)S(1)}, f32[256,128]{1,0:T(8,128)S(1)}, u32[]{:S(2)}, u32[]{:S(2)}) collective-permute-start(f32[256,128]{1,0:T(8,128)S(1)} %get-tuple-element.26), channel_id=1, source_target_pairs={{0,2},{1,3},{2,0},{3,1},{4,6},{5,7},{6,4},{7,5},{8,16},{9,17},{10,... | collective-permute-start | bytes 393224 | tf_op jit(solution)/shard_map/ppermute | solution.py:38
  29.2 10.1 %collective-permute-start.12 = (f32[256,128]{1,0:T(8,128)S(1)}, f32[256,128]{1,0:T(8,128)S(1)}, u32[]{:S(2)}, u32[]{:S(2)}) collective-permute-start(f32[256,128]{1,0:T(8,128)S(1)} %get-tuple-element.27), channel_id=1, source_target_pairs={{0,2},{1,3},{2,0},{3,1},{4,6},{5,7},{6,4},{7,5},{8,17},{9,16},{10,... | collective-permute-start | bytes 393224 | tf_op jit(solution)/shard_map/ppermute | solution.py:38
  31.1 8.2 %collective-permute-start.13 = (f32[256,128]{1,0:T(8,128)S(1)}, f32[256,128]{1,0:T(8,128)S(1)}, u32[]{:S(2)}, u32[]{:S(2)}) collective-permute-start(f32[256,128]{1,0:T(8,128)S(1)} %get-tuple-element.28), channel_id=1, source_target_pairs={{0,2},{1,3},{2,0},{3,1},{4,6},{5,7},{6,4},{7,5},{8,16},{9,18},{10,... | collective-permute-start | bytes 393224 | tf_op jit(solution)/shard_map/ppermute | solution.py:38
  33.8 7.7 %collective-permute-start.9 = (f32[256,128]{1,0:T(8,128)S(1)}, f32[256,128]{1,0:T(8,128)S(1)}, u32[]{:S(2)}, u32[]{:S(2)}) collective-permute-start(f32[256,128]{1,0:T(8,128)S(1)} %get-tuple-element.24), channel_id=1, source_target_pairs={{0,1},{1,0},{2,3},{3,2},{4,5},{5,4},{6,7},{7,6},{8,9},{9,8},{10,11... | collective-permute-start | bytes 393224 | tf_op jit(solution)/shard_map/ppermute | solution.py:38
  34.9 6.5 %collective-permute-start.10 = (f32[256,128]{1,0:T(8,128)S(1)}, f32[256,128]{1,0:T(8,128)S(1)}, u32[]{:S(2)}, u32[]{:S(2)}) collective-permute-start(f32[256,128]{1,0:T(8,128)S(1)} %get-tuple-element.25), channel_id=1, source_target_pairs={{0,8},{1,2},{2,1},{3,4},{4,3},{5,6},{6,5},{7,15},{8,0},{9,10},{10,... | collective-permute-start | bytes 393224 | tf_op jit(solution)/shard_map/ppermute | solution.py:38
  42.0 6.6 %collective-permute-start.21 = (f32[256,128]{1,0:T(8,128)S(1)}, f32[256,128]{1,0:T(8,128)S(1)}, u32[]{:S(2)}, u32[]{:S(2)}) collective-permute-start(f32[256,128]{1,0:T(8,128)S(1)} %shard_map.69.refs_0_.field_ref), channel_id=1, source_target_pairs={{0,2},{1,3},{2,0},{3,1},{4,6},{5,7},{6,4},{7,5},{8,16},{9,18},{10,... | collective-permute-start | bytes 393224 | tf_op jit(solution)/shard_map/ppermute | solution.py:38
  44.2 6.0 %collective-permute-start.15 = (f32[256,128]{1,0:T(8,128)S(1)}, f32[256,128]{1,0:T(8,128)S(1)}, u32[]{:S(2)}, u32[]{:S(2)}) collective-permute-start(f32[256,128]{1,0:T(8,128)S(1)} %shard_map.69.refs_0_.field_ref), channel_id=1, source_target_pairs={{0,8},{1,2},{2,1},{3,4},{4,3},{5,6},{6,5},{7,15},{8,0},{9,10},{10,... | collective-permute-start | bytes 393224 | tf_op jit(solution)/shard_map/ppermute | solution.py:38
  45.5 6.0 %collective-permute-start.14 = (f32[256,128]{1,0:T(8,128)S(1)}, f32[256,128]{1,0:T(8,128)S(1)}, u32[]{:S(2)}, u32[]{:S(2)}) collective-permute-start(f32[256,128]{1,0:T(8,128)S(1)} %shard_map.69.refs_0_.field_ref), channel_id=1, source_target_pairs={{0,1},{1,0},{2,3},{3,2},{4,5},{5,4},{6,7},{7,6},{8,9},{9,8},{10,11... | collective-permute-start | bytes 393224 | tf_op jit(solution)/shard_map/ppermute | solution.py:38
  47.0 8.3 %collective-permute-start.20 = (f32[256,128]{1,0:T(8,128)S(1)}, f32[256,128]{1,0:T(8,128)S(1)}, u32[]{:S(2)}, u32[]{:S(2)}) collective-permute-start(f32[256,128]{1,0:T(8,128)S(1)} %shard_map.69.refs_0_.field_ref), channel_id=1, source_target_pairs={{0,2},{1,3},{2,0},{3,1},{4,6},{5,7},{6,4},{7,5},{8,17},{9,16},{10,... | collective-permute-start | bytes 393224 | tf_op jit(solution)/shard_map/ppermute | solution.py:38
  47.1 8.2 %collective-permute-start.19 = (f32[256,128]{1,0:T(8,128)S(1)}, f32[256,128]{1,0:T(8,128)S(1)}, u32[]{:S(2)}, u32[]{:S(2)}) collective-permute-start(f32[256,128]{1,0:T(8,128)S(1)} %shard_map.69.refs_0_.field_ref), channel_id=1, source_target_pairs={{0,2},{1,3},{2,0},{3,1},{4,6},{5,7},{6,4},{7,5},{8,16},{9,17},{10,... | collective-permute-start | bytes 393224 | tf_op jit(solution)/shard_map/ppermute | solution.py:38
  48.7 6.6 %collective-permute-start.16 = (f32[256,128]{1,0:T(8,128)S(1)}, f32[256,128]{1,0:T(8,128)S(1)}, u32[]{:S(2)}, u32[]{:S(2)}) collective-permute-start(f32[256,128]{1,0:T(8,128)S(1)} %shard_map.69.refs_0_.field_ref), channel_id=1, source_target_pairs={{0,8},{1,9},{2,10},{3,11},{4,12},{5,13},{6,14},{7,15},{8,0},{9,1},... | collective-permute-start | bytes 393224 | tf_op jit(solution)/shard_map/ppermute | solution.py:38
  63.2 5.2 %collective-permute-start.22 = (f32[2,128,384]{2,1,0:T(8,128)S(1)}, f32[2,128,384]{2,1,0:T(8,128)S(1)}, u32[]{:S(2)}, u32[]{:S(2)}) collective-permute-start(f32[2,128,384]{2,1,0:T(8,128)S(1)} %get-tuple-element.30), channel_id=1, source_target_pairs={{0,8},{1,9},{2,10},{3,11},{4,12},{5,13},{6,14},{7,15},{8,0},{9,1},... | collective-permute-start | bytes 1179656 | tf_op jit(solution)/shard_map/ppermute | solution.py:38
  63.3 7.5 %collective-permute-start.25 = (f32[256,128]{1,0:T(8,128)S(1)}, f32[256,128]{1,0:T(8,128)S(1)}, u32[]{:S(2)}, u32[]{:S(2)}) collective-permute-start(f32[256,128]{1,0:T(8,128)S(1)} %get-tuple-element.34), channel_id=1, source_target_pairs={{0,2},{1,3},{2,0},{3,1},{4,6},{5,7},{6,4},{7,5},{8,16},{9,17},{10,... | collective-permute-start | bytes 393224 | tf_op jit(solution)/shard_map/ppermute | solution.py:38
  64.2 7.1 %collective-permute-start.26 = (f32[256,128]{1,0:T(8,128)S(1)}, f32[256,128]{1,0:T(8,128)S(1)}, u32[]{:S(2)}, u32[]{:S(2)}) collective-permute-start(f32[256,128]{1,0:T(8,128)S(1)} %get-tuple-element.35), channel_id=1, source_target_pairs={{0,2},{1,3},{2,0},{3,1},{4,6},{5,7},{6,4},{7,5},{8,17},{9,16},{10,... | collective-permute-start | bytes 393224 | tf_op jit(solution)/shard_map/ppermute | solution.py:38
  66.8 6.3 %collective-permute-start.27 = (f32[256,128]{1,0:T(8,128)S(1)}, f32[256,128]{1,0:T(8,128)S(1)}, u32[]{:S(2)}, u32[]{:S(2)}) collective-permute-start(f32[256,128]{1,0:T(8,128)S(1)} %get-tuple-element.36), channel_id=1, source_target_pairs={{0,2},{1,3},{2,0},{3,1},{4,6},{5,7},{6,4},{7,5},{8,16},{9,18},{10,... | collective-permute-start | bytes 393224 | tf_op jit(solution)/shard_map/ppermute | solution.py:38
  69.0 8.5 %collective-permute-start.23 = (f32[256,128]{1,0:T(8,128)S(1)}, f32[256,128]{1,0:T(8,128)S(1)}, u32[]{:S(2)}, u32[]{:S(2)}) collective-permute-start(f32[256,128]{1,0:T(8,128)S(1)} %get-tuple-element.32), channel_id=1, source_target_pairs={{0,1},{1,0},{2,3},{3,2},{4,5},{5,4},{6,7},{7,6},{8,9},{9,8},{10,11... | collective-permute-start | bytes 393224 | tf_op jit(solution)/shard_map/ppermute | solution.py:38
  69.1 8.5 %collective-permute-start.24 = (f32[256,128]{1,0:T(8,128)S(1)}, f32[256,128]{1,0:T(8,128)S(1)}, u32[]{:S(2)}, u32[]{:S(2)}) collective-permute-start(f32[256,128]{1,0:T(8,128)S(1)} %get-tuple-element.33), channel_id=1, source_target_pairs={{0,8},{1,2},{2,1},{3,4},{4,3},{5,6},{6,5},{7,15},{8,0},{9,10},{10,... | collective-permute-start | bytes 393224 | tf_op jit(solution)/shard_map/ppermute | solution.py:38
  (10 other events, 67.8 us)
